TPU v7x, 128 devices: a whole 4x4x4 slice. The times are simulated.
128 devices in a mesh: hid: 16 (over x, y), wid: 4 (over z_lo, core), rep: 2 (over z_hi).
Axes of the slice: x: 4, y: 4, z: 4 (z_hi: 2, z_lo: 2; z = z_hi * 2 + z_lo), core: 2. Of those that a mesh axis runs over, the one named last changes fastest.
Arguments:
- grad_out: bfloat16 [2, 1024, 8192], P('rep', None, 'wid'), may hold values from -6 to 6
- down_weight: bfloat16 [28672, 8192], P('hid', 'wid'), may hold values from -0.03125 to 0.03125
- saved_gate: bfloat16 [2, 1024, 28672], P('rep', 'wid', 'hid'), may hold values from -6 to 6
- saved_up: bfloat16 [2, 1024, 28672], P('rep', 'wid', 'hid'), may hold values from -6 to 6
- saved_codes: int32 [2, 1024, 28672], P('rep', 'wid', 'hid'), may hold values from -128 to 127, as said below
- exponents: int32 [2, 1024, 224], P('rep', 'wid', 'hid'), may hold values from -12 to -9
Outputs:
- grad_gate: bfloat16 [2, 1024, 28672], P('rep', 'wid', 'hid')
- grad_up: bfloat16 [2, 1024, 28672], P('rep', 'wid', 'hid')
- grad_down: float32 [28672, 8192], P('hid', ('wid', 'rep'))
Inputs may be any that keep to these rules, and one draw needn't show every extreme that they name: `saved_codes`: codes at the clip limits -128 and 127 both occur.
All inputs are finite; a program needn't handle non-finite values.
Results may differ from a plain program's by a relative error of at most 0.014.
Values may be sent and summed in bfloat16 or wider, within the bound.
No kernel may reach another device: no remote copies, remote signals or barrier semaphores. Data moves between devices by JAX's collectives and lax.ppermute only.
A program may use at most 128 MiB of HBM per device.

v0:
```python
import math
import jax
import jax.numpy as jnp
from jax import lax
from jax.sharding import PartitionSpec as P

BLOCK = 128


def from_partner(block, axis, distance):
    count = lax.axis_size(axis)
    route = []
    for low in range(count):
        high = low | 1 << distance
        if high != low and high < count:
            route += [(low, high), (high, low)]
    return lax.ppermute(block, axis, route)


def sylvester(order):
    indices = jnp.arange(order, dtype=jnp.int32)
    both = jnp.bitwise_and(indices[:, None], indices[None, :])
    parity = jnp.zeros((order, order), jnp.int32)
    for bit_index in range(order.bit_length() - 1):
        parity = jnp.bitwise_xor(parity, jnp.bitwise_and(jnp.right_shift(both, bit_index), 1))
    return (1 - 2 * parity).astype(jnp.float32)


def block_transform(values, order):
    tok_local, hidden_local = values.shape
    table_block = sylvester(order) / math.sqrt(order)
    shaped = values.reshape(tok_local, hidden_local // order, order)
    shaped = jnp.einsum("tbk,kj->tbj", shaped, table_block, precision=lax.Precision.HIGHEST)
    return shaped.reshape(tok_local, hidden_local)


def shards(grad_out, down_weight, saved_gate, saved_up, saved_codes, exponents):
    out_rows = grad_out[0]
    codes_local = saved_codes[0]
    tok_local, hidden_local = codes_local.shape
    block_count = hidden_local // BLOCK
    scales = jnp.exp2(exponents[0].astype(jnp.float32))
    dequant = (
        (
            codes_local.astype(jnp.float32).reshape(tok_local, block_count, BLOCK)
            * scales[:, :, None]
        )
        .reshape(tok_local, hidden_local)
        .astype(jnp.bfloat16)
    )
    rows = out_rows
    grad_quant = lax.psum_scatter(
        lax.dot_general(
            rows, down_weight, (((1,), (1,)), ((), ())), preferred_element_type=jnp.float32
        ).astype(jnp.bfloat16),
        "wid",
        scatter_dimension=0,
        tiled=True,
    ).astype(jnp.float32)
    keep_mask = (codes_local > -128) & (codes_local < 127)
    masked = jnp.where(keep_mask, grad_quant, jnp.float32(0.0))
    mixed = block_transform(masked, BLOCK)
    group_count = lax.axis_size("hid")
    position = lax.axis_index("hid")
    for bit_index in range(group_count.bit_length() - 1):
        partner = from_partner(mixed.astype(jnp.bfloat16), "hid", bit_index).astype(mixed.dtype)
        upper = jnp.bitwise_and(jnp.right_shift(position, bit_index), 1) == 1
        mixed = jnp.where(upper, partner - mixed, mixed + partner)
    grad_hidden = mixed * (1.0 / math.sqrt(group_count))
    gate_local = saved_gate[0].astype(jnp.float32)
    up_local = saved_up[0].astype(jnp.float32)
    sigmoid_gate = jax.nn.sigmoid(gate_local)
    grad_gate = (
        grad_hidden * up_local * sigmoid_gate * (1.0 + gate_local * (1.0 - sigmoid_gate))
    ).astype(jnp.bfloat16)
    grad_up = (grad_hidden * gate_local * sigmoid_gate).astype(jnp.bfloat16)
    rows = out_rows
    replica_term = lax.dot_general(
        lax.all_gather(dequant, "wid", axis=0, tiled=True),
        rows,
        (((0,), (0,)), ((), ())),
        preferred_element_type=jnp.float32,
    )
    grad_down = lax.psum_scatter(
        replica_term.astype(jnp.bfloat16), "rep", scatter_dimension=1, tiled=True
    ).astype(jnp.float32)
    return (grad_gate[None], grad_up[None], grad_down)


def solution(mesh):
    in_specs = (
        P("rep", None, "wid"),
        P("hid", "wid"),
        P("rep", "wid", "hid"),
        P("rep", "wid", "hid"),
        P("rep", "wid", "hid"),
        P("rep", "wid", "hid"),
    )
    out_specs = (P("rep", "wid", "hid"), P("rep", "wid", "hid"), P("hid", ("wid", "rep")))
    return jax.shard_map(shards, mesh=mesh, in_specs=in_specs, out_specs=out_specs, check_vma=False)
```

profile of v0, /device:TPU:0, one launch (start us, length us, event | category | flops | bytes accessed | tf_op | source)
XLA Modules:
  0.0 223.2 jit_solution(2910662900731102619)
XLA Ops:
  7.2 0.0 copy-start.2
  7.2 0.0 all-gather.2.cloned.1.call-start
  7.2 1.8 copy.19
  9.0 0.0 copy-done.2
  9.1 1.1 fusion.20
  10.2 0.0 all-gather.2.cloned.1.call-update
  10.2 0.0 reduce-scatter.3.cloned.1.call-start
  10.3 13.0 %fusion.3 = bf16[1024,1792]{1,0:T(8,128)(2,1)} fusion(bf16[1792,2048]{1,0:T(8,128)(2,1)} %param.7, bf16[1,1024,2048]{2,1,0:T(8,128)(2,1)} %param.6), kind=kOutput, calls=%fused_computation.4 | convolution fusion | flops 7518027776 | bytes 15204352 | tf_op jit(solution)/shard_map/dot_general | solution.py:53
  23.2 0.0 reduce-scatter.3.cloned.1.call-update
  23.3 0.0 reduce-scatter.5.cloned.1.call-start
  23.3 31.0 %all-gather.2.cloned.1.call-done = bf16[1024,1792]{0,1:T(8,128)(2,1)} async-done(((bf16[256,1792]{0,1:T(8,128)(2,1)}), bf16[1024,1792]{0,1:T(8,128)(2,1)}) %all-gather.2.cloned.1.call-update) | async-done | bytes 3670032 | tf_op jit(solution)/shard_map/all_gather | solution.py:79
  54.4 12.5 %convolution_convert_fusion = bf16[1792,2048]{1,0:T(8,128)(2,1)} fusion(bf16[1024,1792]{0,1:T(8,128)(2,1)} %all-gather.2.cloned.1.call-done, bf16[1,1024,2048]{2,1,0:T(8,128)(2,1)} %param.6), kind=kOutput, calls=%fused_computation | convolution fusion | flops 7519862784 | bytes 15204352 | tf_op jit(solution)/shard_map/dot_general | solution.py:78
  66.9 0.0 copy-start.1
  66.9 0.0 reduce-scatter.5.cloned.1.call-update
  66.9 32.4 %reduce-scatter.3.cloned.1.call-done = bf16[256,1792]{1,0:T(8,128)(2,1)} async-done(((bf16[1024,1792]{1,0:T(8,128)(2,1)}), bf16[256,1792]{1,0:T(8,128)(2,1)}) %reduce-scatter.3.cloned.1.call-update) | async-done | bytes 917520 | tf_op jit(solution)/shard_map/reduce_scatter | solution.py:52
  99.3 0.0 copy-done.1
  99.3 2.7 %convert_select_fusion = f32[256,1792]{1,0:T(8,128)} fusion(bf16[256,1792]{1,0:T(8,128)(2,1)} %reduce-scatter.3.cloned.1.call-done, s32[1,256,1792]{2,1,0:T(8,128)S(1)} %copy-done.1), kind=kLoop, calls=%fused_computation.33 | loop fusion | flops 2293760 | bytes 4587520 | tf_op jit(solution)/shard_map/jit(_where)/select_n | solution.py:61
  102.1 1.8 copy.14
  103.9 3.1 %fusion.25 = f32[256,14,128]{0,2,1:T(8,128)} fusion(f32[256,14,128]{0,2,1:T(8,128)S(1)} %bitcast.43), kind=kOutput, calls=%fused_computation.38 | convolution fusion | flops 705052672 | bytes 3670016 | tf_op jit(solution)/shard_map/tbk,kj->tbj/dot_general | solution.py:33
  107.0 1.8 copy.16
  108.8 1.0 convert_element_type.79
  109.8 1.5 collective-permute-start
  111.3 21.2 %collective-permute-done = bf16[256,1792]{1,0:T(8,128)(2,1)S(1)} collective-permute-done((bf16[256,1792]{1,0:T(8,128)(2,1)}, bf16[256,1792]{1,0:T(8,128)(2,1)S(1)}, u32[]{:S(2)}, u32[]{:S(2)}) %collective-permute-start) | collective-permute-done | bytes 917536 | tf_op jit(solution)/shard_map/ppermute | solution.py:17
  132.4 1.2 fusion.22
  133.6 3.0 %collective-permute-start.1 = (bf16[256,1792]{1,0:T(8,128)(2,1)}, bf16[256,1792]{1,0:T(8,128)(2,1)}, u32[]{:S(2)}, u32[]{:S(2)}) collective-permute-start(bf16[256,1792]{1,0:T(8,128)(2,1)} %fusion.22), channel_id=1, source_target_pairs={{0,16},{16,0},{8,24},{24,8},{32,48},{48,32},{40,56},{56,40},{64,80... | collective-permute-start | bytes 2752520 | tf_op jit(solution)/shard_map/ppermute | solution.py:17
  136.6 20.5 %collective-permute-done.1 = bf16[256,1792]{1,0:T(8,128)(2,1)} collective-permute-done((bf16[256,1792]{1,0:T(8,128)(2,1)}, bf16[256,1792]{1,0:T(8,128)(2,1)}, u32[]{:S(2)}, u32[]{:S(2)}) %collective-permute-start.1) | collective-permute-done | bytes 917536 | tf_op jit(solution)/shard_map/ppermute | solution.py:17
  157.1 3.2 %fusion.70 = (bf16[256,1792]{1,0:T(8,128)(2,1)}, f32[256,1792]{1,0:T(8,128)}) fusion(f32[256,1792]{1,0:T(8,128)S(1)} %copy.16, bf16[256,1792]{1,0:T(8,128)(2,1)S(1)} %collective-permute-done, pred[]{:T(512)S(6)} %eq.15, bf16[256,1792]{1,0:T(8,128)(2,1)} %collective-permute-done.1, pred[]{:T(512)S(6)} %eq.14), kind=kLoop, calls=%fused_computation.85 | loop fusion | flops 4128768 | bytes 6422530 | tf_op jit(solution)/shard_map/convert_element_type | solution.py:66
  160.3 1.5 collective-permute-start.2
  161.8 19.7 %collective-permute-done.2 = bf16[256,1792]{1,0:T(8,128)(2,1)S(1)} collective-permute-done((bf16[256,1792]{1,0:T(8,128)(2,1)}, bf16[256,1792]{1,0:T(8,128)(2,1)S(1)}, u32[]{:S(2)}, u32[]{:S(2)}) %collective-permute-start.2) | collective-permute-done | bytes 917536 | tf_op jit(solution)/shard_map/ppermute | solution.py:17
  181.5 0.0 copy-start
  181.5 2.8 %fusion.21 = bf16[256,1792]{1,0:T(8,128)(2,1)} fusion(f32[256,1792]{1,0:T(8,128)} %get-tuple-element.4, bf16[256,1792]{1,0:T(8,128)(2,1)S(1)} %collective-permute-done.2, pred[]{:T(512)S(6)} %eq.13), kind=kLoop, calls=%fused_computation.34 | loop fusion | flops 2293760 | bytes 3670017 | tf_op jit(solution)/shard_map/convert_element_type | solution.py:66
  184.3 3.0 %collective-permute-start.3 = (bf16[256,1792]{1,0:T(8,128)(2,1)}, bf16[256,1792]{1,0:T(8,128)(2,1)}, u32[]{:S(2)}, u32[]{:S(2)}) collective-permute-start(bf16[256,1792]{1,0:T(8,128)(2,1)} %fusion.21), channel_id=1, source_target_pairs={{0,64},{64,0},{8,72},{72,8},{16,80},{80,16},{24,88},{88,24},{32,96... | collective-permute-start | bytes 2752520 | tf_op jit(solution)/shard_map/ppermute | solution.py:17
  187.3 19.0 %collective-permute-done.3 = bf16[256,1792]{1,0:T(8,128)(2,1)} collective-permute-done((bf16[256,1792]{1,0:T(8,128)(2,1)}, bf16[256,1792]{1,0:T(8,128)(2,1)}, u32[]{:S(2)}, u32[]{:S(2)}) %collective-permute-start.3) | collective-permute-done | bytes 917536 | tf_op jit(solution)/shard_map/ppermute | solution.py:17
  206.4 0.0 copy-done
  206.4 4.4 %fusion.23 = (bf16[1,256,1792]{2,1,0:T(8,128)(2,1)}, bf16[1,256,1792]{2,1,0:T(8,128)(2,1)}) fusion(bf16[1,256,1792]{2,1,0:T(8,128)(2,1)} %param.8, f32[256,1792]{1,0:T(8,128)S(1)} %copy-done, bf16[256,1792]{1,0:T(8,128)(2,1)S(1)} %collective-permute-done.2, pred[]{:T(512)S(6)} %eq.13, bf16[256,1792]{1,0:T(8,128)(2,1)} %collective-permute-done.3, ...), kind=kLoop, calls=%fused_computation.36 | loop fusion | flops 11010048 | bytes 7340034 | tf_op jit(solution)/shard_map/broadcast_in_dim | solution.py:87
  210.7 0.0 reduce-scatter.5.cloned.1.call-done
  210.7 6.0 %convert_element_type.98 = f32[1792,1024]{1,0:T(8,128)} convert(bf16[1792,1024]{1,0:T(8,128)(2,1)} %reduce-scatter.5.cloned.1.call-done) | non-fusion elementwise | flops 1835008 | bytes 11010048 | tf_op jit(solution)/shard_map/convert_element_type | solution.py:86
  (2 shorter events, 0.0 us)
Async XLA Ops:
  7.2 1.9 copy-start.2
  7.2 47.2 %all-gather.2.cloned.1.call-start = ((), (), s32[]{:S(2)}) async-start(), calls=%async_computation.3 | async-start | bytes 4587520 | tf_op jit(solution)/shard_map/all_gather | solution.py:79
  10.2 89.1 %reduce-scatter.3.cloned.1.call-start = ((), (), s32[]{:S(2)}) async-start(), calls=%async_computation.2 | async-start | bytes 4587520 | tf_op jit(solution)/shard_map/reduce_scatter | solution.py:52
  23.3 187.5 %reduce-scatter.5.cloned.1.call-start = ((), (), s32[]{:S(2)}) async-start(), calls=%async_computation.4 | async-start | bytes 11010048 | tf_op jit(solution)/shard_map/reduce_scatter | solution.py:84
  66.9 32.5 %copy-start.1 = (s32[1,256,1792]{2,1,0:T(8,128)S(1)}, s32[1,256,1792]{2,1,0:T(8,128)}, u32[]{:S(2)}) copy-start(s32[1,256,1792]{2,1,0:T(8,128)} %param.10) | copy-start | bytes 5505028
  109.8 22.6 %collective-permute-start = (bf16[256,1792]{1,0:T(8,128)(2,1)}, bf16[256,1792]{1,0:T(8,128)(2,1)S(1)}, u32[]{:S(2)}, u32[]{:S(2)}) collective-permute-start(bf16[256,1792]{1,0:T(8,128)(2,1)} %convert_element_type.79), channel_id=1, source_target_pairs={{0,8},{8,0},{16,24},{24,16},{32,40},{40,32},{48,56},{56,48},{64,72... | collective-permute-start | bytes 2752520 | tf_op jit(solution)/shard_map/ppermute | solution.py:17
  133.6 23.5 %collective-permute-start.1 = (bf16[256,1792]{1,0:T(8,128)(2,1)}, bf16[256,1792]{1,0:T(8,128)(2,1)}, u32[]{:S(2)}, u32[]{:S(2)}) collective-permute-start(bf16[256,1792]{1,0:T(8,128)(2,1)} %fusion.22), channel_id=1, source_target_pairs={{0,16},{16,0},{8,24},{24,8},{32,48},{48,32},{40,56},{56,40},{64,80... | collective-permute-start | bytes 2752520 | tf_op jit(solution)/shard_map/ppermute | solution.py:17
  160.3 21.2 %collective-permute-start.2 = (bf16[256,1792]{1,0:T(8,128)(2,1)}, bf16[256,1792]{1,0:T(8,128)(2,1)S(1)}, u32[]{:S(2)}, u32[]{:S(2)}) collective-permute-start(bf16[256,1792]{1,0:T(8,128)(2,1)} %get-tuple-element.3), channel_id=1, source_target_pairs={{0,32},{32,0},{8,40},{40,8},{16,48},{48,16},{24,56},{56,24},{64,96... | collective-permute-start | bytes 2752520 | tf_op jit(solution)/shard_map/ppermute | solution.py:17
  181.5 24.8 %copy-start = (f32[256,1792]{1,0:T(8,128)S(1)}, f32[256,1792]{1,0:T(8,128)}, u32[]{:S(2)}) copy-start(f32[256,1792]{1,0:T(8,128)} %get-tuple-element.4) | copy-start | bytes 5505028
  184.3 22.0 %collective-permute-start.3 = (bf16[256,1792]{1,0:T(8,128)(2,1)}, bf16[256,1792]{1,0:T(8,128)(2,1)}, u32[]{:S(2)}, u32[]{:S(2)}) collective-permute-start(bf16[256,1792]{1,0:T(8,128)(2,1)} %fusion.21), channel_id=1, source_target_pairs={{0,64},{64,0},{8,72},{72,8},{16,80},{80,16},{24,88},{88,24},{32,96... | collective-permute-start | bytes 2752520 | tf_op jit(solution)/shard_map/ppermute | solution.py:17
Sparse Core Ops, SparseCore 0:
  10.3 43.9 all-gather.1
  56.8 42.5 reduce-scatter.2
  102.3 93.6 reduce-scatter.4
where the time goes:
time: 224 us; the launch traced here: 223 us
  waiting for transfers between devices  144 us (64%)
  matrix products  28.6 us (13%)
  other arithmetic  22.5 us (10%)
  between operations  13.8 us (6%)
  starting transfers between devices  9.1 us (4%)
  local copies, waits for them, and re-layouts  5.44 us (2%)
    ppermute x4, waiting for transfers between devices, from_partner(): return lax.ppermute(block, axis, route)  80.3 us
    reduce_scatter x1, waiting for transfers between devices, shards(): lax.psum_scatter(lax.dot_general(rows, down_weight, (((1,), (1,)), ((), (...  32.4 us
    all_gather x1, waiting for transfers between devices, shards(): lax.all_gather(dequant, 'wid', axis=0, tiled=True)  31 us
    dot_general x1, matrix products, shards(): lax.dot_general(rows, down_weight, (((1,), (1,)), ((), ())), preferred_el...  13 us
    dot_general x1, matrix products, shards(): lax.dot_general(lax.all_gather(dequant, 'wid', axis=0, tiled=True), rows,...  12.5 us
    ppermute x4, starting transfers between devices, from_partner(): return lax.ppermute(block, axis, route)  8.98 us
    convert_element_type x4, other arithmetic, shards(): mixed.astype(jnp.bfloat16)  8.26 us
    convert_element_type x1, other arithmetic, shards(): grad_down = lax.psum_scatter(replica_term.astype(jnp.bfloat16), 'rep', sc...  5.98 us
  transfers between devices with their start and end apart: 7, of which 6 were waited for; matrix products, arithmetic and copies ran while one was open for 21% of the time, Pallas kernels for 0%

commit v1 on v0

--- a/solution.py
+++ b/solution.py
@@ -5,6 +5,15 @@
 from jax.sharding import PartitionSpec as P
 
 BLOCK = 128
+quotas_trace = lambda chunk: jnp.concatenate(
+    lax.all_to_all(
+        jnp.stack([chunk] * lax.axis_size("wid"), axis=0),
+        axis_name="wid",
+        split_axis=0,
+        concat_axis=0,
+    ),
+    axis=0,
+)
 
 
 def from_partner(block, axis, distance):
@@ -76,10 +85,7 @@
     grad_up = (grad_hidden * gate_local * sigmoid_gate).astype(jnp.bfloat16)
     rows = out_rows
     replica_term = lax.dot_general(
-        lax.all_gather(dequant, "wid", axis=0, tiled=True),
-        rows,
-        (((0,), (0,)), ((), ())),
-        preferred_element_type=jnp.float32,
+        quotas_trace(dequant), rows, (((0,), (0,)), ((), ())), preferred_element_type=jnp.float32
     )
     grad_down = lax.psum_scatter(
         replica_term.astype(jnp.bfloat16), "rep", scatter_dimension=1, tiled=True

time: 224 us -> 236 us (1.054)
  blocking collectives: 0 us -> 74.3 us
  waiting for transfers between devices: 144 us -> 79 us
  local copies, waits for them, and re-layouts: 5.44 us -> 9.51 us
  matrix products: 28.6 us -> 26.2 us
    all_to_all x0 -> x1, blocking collectives: none -> 74.3 us  [lax.all_to_all(jnp.stack([chunk] * lax.axis_size('wid'), axis=0), axis_na...]
    reduce_scatter x1, waiting for transfers between devices: 32.4 us -> 0.02 us  [shards(): lax.psum_scatter(lax.dot_general(rows, down_weight, (((1,), (1,)), ((), (...]
    all_gather x1 -> x0, waiting for transfers between devices: 31 us -> none  [shards(): lax.all_gather(dequant, 'wid', axis=0, tiled=True)]
    another operation x0 -> x2, local copies, waits for them, and re-layouts: none -> 2.79 us  [jnp.stack([chunk] * lax.axis_size('wid'), axis=0)]
    dot_general x1, matrix products: 12.5 us -> 10.1 us  [shards(): lax.dot_general(quotas_trace(dequant), rows, (((0,), (0,)), ((), ())), pr...]
  transfers between devices with their start and end apart: 7 -> 6, of which waited for: 6 -> 4; matrix products, arithmetic and copies ran while one was open for 21% -> 16% of each run, Pallas kernels for 0% -> 0%
where the time goes in v1:
time: 236 us; the launch traced here: 235 us
  waiting for transfers between devices  79 us (33%)
  blocking collectives  74.3 us (31%)
  matrix products  26.2 us (11%)
  other arithmetic  23 us (10%)
  between operations  14.1 us (6%)
  local copies, waits for them, and re-layouts  9.51 us (4%)
  starting transfers between devices  9.04 us (4%)
    ppermute x4, waiting for transfers between devices, from_partner(): return lax.ppermute(block, axis, route)  79 us
    all_to_all x1, blocking collectives, lax.all_to_all(jnp.stack([chunk] * lax.axis_size('wid'), axis=0), axis_na...  74.3 us
    dot_general x1, matrix products, shards(): lax.dot_general(rows, down_weight, (((1,), (1,)), ((), ())), preferred_el...  13 us
    dot_general x1, matrix products, shards(): lax.dot_general(quotas_trace(dequant), rows, (((0,), (0,)), ((), ())), pr...  10.1 us
    ppermute x4, starting transfers between devices, from_partner(): return lax.ppermute(block, axis, route)  8.96 us
    convert_element_type x4, other arithmetic, shards(): mixed.astype(jnp.bfloat16)  8.24 us
    convert_element_type x1, other arithmetic, shards(): grad_down = lax.psum_scatter(replica_term.astype(jnp.bfloat16), 'rep', sc...  5.98 us
  transfers between devices with their start and end apart: 6, of which 4 were waited for; matrix products, arithmetic and copies ran while one was open for 16% of the time, Pallas kernels for 0%

profile of v1, /device:TPU:0, one launch (start us, length us, event | category | flops | bytes accessed | tf_op | source)
XLA Modules:
  0.0 235.2 jit_solution(9088038018615069820)
XLA Ops:
  7.2 0.0 reduce-scatter.3.cloned.1.call-start
  7.2 13.0 %fusion.3 = bf16[1024,1792]{1,0:T(8,128)(2,1)} fusion(bf16[1792,2048]{1,0:T(8,128)(2,1)} %param.7, bf16[1,1024,2048]{2,1,0:T(8,128)(2,1)} %param.6), kind=kOutput, calls=%fused_computation.4 | convolution fusion | flops 7518027776 | bytes 15204352 | tf_op jit(solution)/shard_map/dot_general | solution.py:62
  20.2 0.0 copy-start.1
  20.2 0.0 reduce-scatter.3.cloned.1.call-update
  20.2 0.0 copy-start.2
  20.2 0.0 reduce-scatter.5.cloned.1.call-start
  20.3 1.4 copy-done.1
  21.7 1.7 copy.19
  23.4 0.0 copy-done.2
  23.4 1.7 fusion.20
  25.1 1.4 copy.20
  26.5 1.4 stack.10
  27.9 0.0 copy-start.3
  27.9 74.3 %all_to_all.5 = bf16[4,256,1792]{2,1,0:T(8,128)(2,1)S(1)} all-to-all(bf16[4,256,1792]{2,1,0:T(8,128)(2,1)S(1)} %stack.10), channel_id=1, replica_groups=mesh['hid'=16,'wid'=4,'rep'=2] {'wid'}, dimensions={0} | all-to-all | bytes 7340032 | tf_op jit(solution)/shard_map/all_to_all | solution.py:9
  102.2 0.0 copy-done.3
  102.2 10.1 %convolution_convert_fusion = bf16[1792,2048]{1,0:T(8,128)(2,1)} fusion(bf16[1024,1792]{1,0:T(8,128)(2,1)S(1)} %bitcast.45, bf16[1,1024,2048]{2,1,0:T(8,128)(2,1)S(1)} %copy-done.3), kind=kOutput, calls=%fused_computation | convolution fusion | flops 7519862784 | bytes 15204352 | tf_op jit(solution)/shard_map/dot_general | solution.py:87
  112.3 0.0 reduce-scatter.5.cloned.1.call-update
  112.3 0.0 reduce-scatter.3.cloned.1.call-done
  112.4 2.8 %convert_select_fusion = f32[256,1792]{1,0:T(8,128)} fusion(bf16[256,1792]{1,0:T(8,128)(2,1)} %reduce-scatter.3.cloned.1.call-done, s32[1,256,1792]{2,1,0:T(8,128)S(1)} %copy-done.1), kind=kLoop, calls=%fused_computation.33 | loop fusion | flops 2293760 | bytes 4587520 | tf_op jit(solution)/shard_map/jit(_where)/select_n | solution.py:70
  115.1 1.8 copy.14
  116.9 3.1 %fusion.25 = f32[256,14,128]{0,2,1:T(8,128)} fusion(f32[256,14,128]{0,2,1:T(8,128)S(1)} %bitcast.43), kind=kOutput, calls=%fused_computation.38 | convolution fusion | flops 705052672 | bytes 3670016 | tf_op jit(solution)/shard_map/tbk,kj->tbj/dot_general | solution.py:42
  120.0 1.8 copy.16
  121.9 1.0 convert_element_type.78
  122.9 1.5 collective-permute-start
  124.4 20.9 %collective-permute-done = bf16[256,1792]{1,0:T(8,128)(2,1)S(1)} collective-permute-done((bf16[256,1792]{1,0:T(8,128)(2,1)}, bf16[256,1792]{1,0:T(8,128)(2,1)S(1)}, u32[]{:S(2)}, u32[]{:S(2)}) %collective-permute-start) | collective-permute-done | bytes 917536 | tf_op jit(solution)/shard_map/ppermute | solution.py:26
  145.2 1.2 fusion.22
  146.4 3.0 %collective-permute-start.1 = (bf16[256,1792]{1,0:T(8,128)(2,1)}, bf16[256,1792]{1,0:T(8,128)(2,1)}, u32[]{:S(2)}, u32[]{:S(2)}) collective-permute-start(bf16[256,1792]{1,0:T(8,128)(2,1)} %fusion.22), channel_id=1, source_target_pairs={{0,16},{16,0},{8,24},{24,8},{32,48},{48,32},{40,56},{56,40},{64,80... | collective-permute-start | bytes 2752520 | tf_op jit(solution)/shard_map/ppermute | solution.py:26
  149.5 20.2 %collective-permute-done.1 = bf16[256,1792]{1,0:T(8,128)(2,1)} collective-permute-done((bf16[256,1792]{1,0:T(8,128)(2,1)}, bf16[256,1792]{1,0:T(8,128)(2,1)}, u32[]{:S(2)}, u32[]{:S(2)}) %collective-permute-start.1) | collective-permute-done | bytes 917536 | tf_op jit(solution)/shard_map/ppermute | solution.py:26
  169.6 3.2 %fusion.70 = (bf16[256,1792]{1,0:T(8,128)(2,1)}, f32[256,1792]{1,0:T(8,128)}) fusion(f32[256,1792]{1,0:T(8,128)S(1)} %copy.16, bf16[256,1792]{1,0:T(8,128)(2,1)S(1)} %collective-permute-done, pred[]{:T(512)S(6)} %eq.15, bf16[256,1792]{1,0:T(8,128)(2,1)} %collective-permute-done.1, pred[]{:T(512)S(6)} %eq.14), kind=kLoop, calls=%fused_computation.85 | loop fusion | flops 4128768 | bytes 6422530 | tf_op jit(solution)/shard_map/convert_element_type | solution.py:75
  172.8 1.5 collective-permute-start.2
  174.3 19.3 %collective-permute-done.2 = bf16[256,1792]{1,0:T(8,128)(2,1)S(1)} collective-permute-done((bf16[256,1792]{1,0:T(8,128)(2,1)}, bf16[256,1792]{1,0:T(8,128)(2,1)S(1)}, u32[]{:S(2)}, u32[]{:S(2)}) %collective-permute-start.2) | collective-permute-done | bytes 917536 | tf_op jit(solution)/shard_map/ppermute | solution.py:26
  193.6 0.0 copy-start
  193.6 2.8 %fusion.21 = bf16[256,1792]{1,0:T(8,128)(2,1)} fusion(f32[256,1792]{1,0:T(8,128)} %get-tuple-element.4, bf16[256,1792]{1,0:T(8,128)(2,1)S(1)} %collective-permute-done.2, pred[]{:T(512)S(6)} %eq.13), kind=kLoop, calls=%fused_computation.34 | loop fusion | flops 2293760 | bytes 3670017 | tf_op jit(solution)/shard_map/convert_element_type | solution.py:75
  196.4 3.0 %collective-permute-start.3 = (bf16[256,1792]{1,0:T(8,128)(2,1)}, bf16[256,1792]{1,0:T(8,128)(2,1)}, u32[]{:S(2)}, u32[]{:S(2)}) collective-permute-start(bf16[256,1792]{1,0:T(8,128)(2,1)} %fusion.21), channel_id=1, source_target_pairs={{0,64},{64,0},{8,72},{72,8},{16,80},{80,16},{24,88},{88,24},{32,96... | collective-permute-start | bytes 2752520 | tf_op jit(solution)/shard_map/ppermute | solution.py:26
  199.4 18.6 %collective-permute-done.3 = bf16[256,1792]{1,0:T(8,128)(2,1)} collective-permute-done((bf16[256,1792]{1,0:T(8,128)(2,1)}, bf16[256,1792]{1,0:T(8,128)(2,1)}, u32[]{:S(2)}, u32[]{:S(2)}) %collective-permute-start.3) | collective-permute-done | bytes 917536 | tf_op jit(solution)/shard_map/ppermute | solution.py:26
  218.0 0.0 copy-done
  218.0 4.4 %fusion.23 = (bf16[1,256,1792]{2,1,0:T(8,128)(2,1)}, bf16[1,256,1792]{2,1,0:T(8,128)(2,1)}) fusion(bf16[1,256,1792]{2,1,0:T(8,128)(2,1)} %param.8, f32[256,1792]{1,0:T(8,128)S(1)} %copy-done, bf16[256,1792]{1,0:T(8,128)(2,1)S(1)} %collective-permute-done.2, pred[]{:T(512)S(6)} %eq.13, bf16[256,1792]{1,0:T(8,128)(2,1)} %collective-permute-done.3, ...), kind=kLoop, calls=%fused_computation.36 | loop fusion | flops 11010048 | bytes 7340034 | tf_op jit(solution)/shard_map/broadcast_in_dim | solution.py:93
  222.4 0.0 reduce-scatter.5.cloned.1.call-done
  222.4 6.0 %convert_element_type.96 = f32[1792,1024]{1,0:T(8,128)} convert(bf16[1792,1024]{1,0:T(8,128)(2,1)} %reduce-scatter.5.cloned.1.call-done) | non-fusion elementwise | flops 1835008 | bytes 11010048 | tf_op jit(solution)/shard_map/convert_element_type | solution.py:92
  (2 shorter events, 0.0 us)
Async XLA Ops:
  7.2 105.2 %reduce-scatter.3.cloned.1.call-start = ((), (), s32[]{:S(2)}) async-start(), calls=%async_computation.3 | async-start | bytes 4587520 | tf_op jit(solution)/shard_map/reduce_scatter | solution.py:61
  20.2 1.5 copy-start.1
  20.2 3.2 %copy-start.2 = (s32[1,256,14]{1,0,2:T(1,128)S(1)}, s32[1,256,14]{1,0,2:T(1,128)}, u32[]{:S(2)}) copy-start(s32[1,256,14]{1,0,2:T(1,128)} %param.11) | copy-start | bytes 43012
  20.2 202.2 %reduce-scatter.5.cloned.1.call-start = ((), (), s32[]{:S(2)}) async-start(), calls=%async_computation.4 | async-start | bytes 11010048 | tf_op jit(solution)/shard_map/reduce_scatter | solution.py:90
  27.9 74.3 %copy-start.3 = (bf16[1,1024,2048]{2,1,0:T(8,128)(2,1)S(1)}, bf16[1,1024,2048]{2,1,0:T(8,128)(2,1)}, u32[]{:S(2)}) copy-start(bf16[1,1024,2048]{2,1,0:T(8,128)(2,1)} %param.6) | copy-start | bytes 12582916
  122.9 22.4 %collective-permute-start = (bf16[256,1792]{1,0:T(8,128)(2,1)}, bf16[256,1792]{1,0:T(8,128)(2,1)S(1)}, u32[]{:S(2)}, u32[]{:S(2)}) collective-permute-start(bf16[256,1792]{1,0:T(8,128)(2,1)} %convert_element_type.78), channel_id=1, source_target_pairs={{0,8},{8,0},{16,24},{24,16},{32,40},{40,32},{48,56},{56,48},{64,72... | collective-permute-start | bytes 2752520 | tf_op jit(solution)/shard_map/ppermute | solution.py:26
  146.4 23.2 %collective-permute-start.1 = (bf16[256,1792]{1,0:T(8,128)(2,1)}, bf16[256,1792]{1,0:T(8,128)(2,1)}, u32[]{:S(2)}, u32[]{:S(2)}) collective-permute-start(bf16[256,1792]{1,0:T(8,128)(2,1)} %fusion.22), channel_id=1, source_target_pairs={{0,16},{16,0},{8,24},{24,8},{32,48},{48,32},{40,56},{56,40},{64,80... | collective-permute-start | bytes 2752520 | tf_op jit(solution)/shard_map/ppermute | solution.py:26
  172.8 20.8 %collective-permute-start.2 = (bf16[256,1792]{1,0:T(8,128)(2,1)}, bf16[256,1792]{1,0:T(8,128)(2,1)S(1)}, u32[]{:S(2)}, u32[]{:S(2)}) collective-permute-start(bf16[256,1792]{1,0:T(8,128)(2,1)} %get-tuple-element.3), channel_id=1, source_target_pairs={{0,32},{32,0},{8,40},{40,8},{16,48},{48,16},{24,56},{56,24},{64,96... | collective-permute-start | bytes 2752520 | tf_op jit(solution)/shard_map/ppermute | solution.py:26
  193.6 24.4 %copy-start = (f32[256,1792]{1,0:T(8,128)S(1)}, f32[256,1792]{1,0:T(8,128)}, u32[]{:S(2)}) copy-start(f32[256,1792]{1,0:T(8,128)} %get-tuple-element.4) | copy-start | bytes 5505028
  196.4 21.6 %collective-permute-start.3 = (bf16[256,1792]{1,0:T(8,128)(2,1)}, bf16[256,1792]{1,0:T(8,128)(2,1)}, u32[]{:S(2)}, u32[]{:S(2)}) collective-permute-start(bf16[256,1792]{1,0:T(8,128)(2,1)} %fusion.21), channel_id=1, source_target_pairs={{0,64},{64,0},{8,72},{72,8},{16,80},{80,16},{24,88},{88,24},{32,96... | collective-permute-start | bytes 2752520 | tf_op jit(solution)/shard_map/ppermute | solution.py:26
Sparse Core Ops, SparseCore 0:
  20.3 71.4 reduce-scatter.2
  112.5 93.6 reduce-scatter.4
